TPU v7x, 32 devices: a whole 2x2x4 slice. The times are simulated.
32 devices in a mesh: view: 4 (over x, core), depth: 8 (over z, y).
Axes of the slice: x: 2, y: 2, z: 4, core: 2. Of those that a mesh axis runs over, the one named last changes fastest.
Arguments:
- features: float32 [4, 8, 32, 3, 4096], P('view', 'depth'), may hold values from -6 to 6
- spacing: float32 [4, 8, 3, 4096], P('view', 'depth'), may hold values from 0.01 to 0.15
- counts: int32 [4, 8, 4096], P('view', 'depth'), may hold values from 0 to 3
- depth_rank: int32 [4, 8], P('view', 'depth'), may hold values from 0 to 7, as said below
- target: float32 [4, 64, 4096], P('view', None, 'depth'), may hold values from 0 to 1
- first_weight: float32 [32, 256], replicated, may hold values from -1 to 1
- first_bias: float32 [256], replicated, may hold values from -3 to 3
- second_weight: float32 [256, 256], replicated, may hold values from -0.375 to 0.375
- second_bias: float32 [256], replicated, may hold values from -3 to 3
- last_weight: float32 [256, 65], replicated, may hold values from -0.375 to 0.375
- last_bias: float32 [65], replicated, may hold values from -3 to 3
Outputs:
- pixels: float32 [4, 64, 4096], P('view', None, 'depth')
- first_update: float32 [32, 256], replicated
- first_shift: float32 [256], replicated
- second_update: float32 [256, 256], replicated
- second_shift: float32 [256], replicated
- last_update: float32 [256, 65], replicated
- last_shift: float32 [65], replicated
Inputs may be any that keep to these rules, and one draw needn't show every extreme that they name: depth_rank[v, d] equals d XOR a number fixed for view group v, so each view group's ranks are a permutation in which every aligned block of 2^k regions takes consecutive positions. Sample slots s with s < counts[v, d, r] are live.
All inputs are finite; a program needn't handle non-finite values.
Results may differ from a plain program's by a relative error of at most 0.0003.
Values sent between devices are 32-bit elements; how exact they have to be, the bound alone decides.
A program may use at most 128 MiB of HBM per device.

v0:
```python
import functools

import jax
import jax.numpy as jnp
from jax import lax
from jax.experimental import pallas as pl
from jax.experimental.pallas import tpu as pltpu
from jax.sharding import PartitionSpec as P

epsilon = 1e-05
PAD = 80
MESH = pl.DeviceIdType.MESH
f32 = jnp.float32
bf16 = jnp.bfloat16


def split(value):
    high = value.astype(bf16)
    low = (value - high.astype(f32)).astype(bf16)
    return high, low


def mm(left, right):
    return lax.dot_general(left, right, (((1,), (0,)), ((), ())), preferred_element_type=f32)


def mm_nt(left, right):
    return lax.dot_general(left, right, (((1,), (1,)), ((), ())), preferred_element_type=f32)


def opticals(raw, channels, spacing, counts, samples, rays):
    out = []
    for s in range(samples):
        logit = raw[channels : channels + 1, s * rays : (s + 1) * rays]
        density = jnp.maximum(logit, 0.0) + jnp.log1p(jnp.exp(-jnp.abs(logit)))
        length = jnp.where(s < counts, spacing[s], 0.0)
        out.append((logit, density * length, length))
    return out


def remote(src, dst, sems, slot, device):
    return pltpu.make_async_remote_copy(
        src_ref=src,
        dst_ref=dst,
        send_sem=sems[0].at[slot],
        recv_sem=sems[1].at[slot],
        device_id=device,
        device_id_type=MESH,
    )


def lanes(value):
    total = value[:, 0:128]
    for lane in range(128, value.shape[1], 128):
        total = total + value[:, lane : lane + 128]
    return total


def block_count(feat, hidden, devices):
    blocks = (hidden + feat + PAD) // 8 * (hidden // 128) + 1
    return -(-blocks // devices) * devices


def prepare(feat, w1_ref, b1_ref, w2_ref, b2_ref, w3_ref, b3_ref, w1s, w2f, w2b, w3f, w3b, cols):
    hidden = w2_ref.shape[0]
    outs = w3_ref.shape[0]
    high, low = split(w1_ref[...])
    bias = b1_ref[...]
    bias_a = bias.astype(bf16).astype(f32)
    bias_b = (bias - bias_a).astype(bf16).astype(f32)
    cols[...] = jnp.zeros_like(cols)
    cols[0:feat, :] = high.astype(f32)
    cols[feat : 2 * feat, :] = high.astype(f32)
    cols[2 * feat : 3 * feat, :] = low.astype(f32)
    cols[3 * feat : 3 * feat + 1, :] = bias_a
    cols[3 * feat + 1 : 3 * feat + 2, :] = bias_b
    cols[3 * feat + 2 : 3 * feat + 3, :] = bias - bias_a - bias_b
    cols[3 * feat + 3 : 3 * feat + 4, :] = b2_ref[...]
    cols[3 * feat + 4 : 3 * feat + 5, 0:outs] = b3_ref[...]
    turned = cols[0:128, :].T
    w1s[...] = turned.astype(bf16)
    cols[:, 0:128] = turned
    for stack, weight in ((w2f, w2_ref[...].T), (w2b, w2_ref[...])):
        high, low = split(weight)
        stack[:, 0:hidden] = high
        stack[:, hidden : 2 * hidden] = high
        stack[:, 2 * hidden : 3 * hidden] = low
    tall = jnp.concatenate([w3_ref[...], jnp.zeros((PAD - outs, hidden), f32)], axis=0)
    high, low = split(tall)
    w3f[0:PAD, :] = high
    w3f[PAD : 2 * PAD, :] = low
    high = high.astype(f32)
    stack = jnp.concatenate(
        [high, high, tall - high, jnp.zeros((256 - 3 * PAD, hidden), f32)], axis=0
    )
    w3b[...] = stack.T.astype(bf16)


def forward_tile(feat, channels, x, spacing, counts, w1s, w2f, w3f, cols, keep_x, keep_h, keep_raw):
    samples = len(spacing)
    rays = spacing[0].shape[1]
    xh, xl = split(x)
    keep_x[0] = xh
    keep_x[1] = xl
    rows = lax.broadcasted_iota(jnp.int32, x.shape, 0)
    ones = jnp.where(rows < 3, 1.0, 0.0).astype(bf16)
    z1 = mm(w1s[...], jnp.concatenate([xh, xl, xh, ones], axis=0))
    h1h, h1l = split(jnp.maximum(z1, 0.0))
    keep_h[0] = h1h
    keep_h[1] = h1l
    z2 = mm(w2f[...], jnp.concatenate([h1h, h1l, h1h], axis=0))
    z2 = z2 + cols[:, 3 * feat + 3 : 3 * feat + 4]
    h2h, h2l = split(jnp.maximum(z2, 0.0))
    keep_h[2] = h2h
    keep_h[3] = h2l
    both = mm(w3f[...], h2h)
    raw = both[0:PAD] + both[PAD:] + mm(w3f[0:PAD, :], h2l)
    raw = raw + cols[0:PAD, 3 * feat + 4 : 3 * feat + 5]
    keep_raw[...] = raw
    before = None
    color = None
    parts = opticals(raw, channels, spacing, counts, samples, rays)
    for s, (_, optical, _) in enumerate(parts):
        weight = 1.0 - jnp.exp(-optical)
        if s:
            weight = jnp.exp(-before) * weight
        shade = weight * jax.nn.sigmoid(raw[0:channels, s * rays : (s + 1) * rays])
        color = shade if s == 0 else color + shade
        before = optical if s == 0 else before + optical
    return color, before


def backward_tile(
    channels, raw, misfit, state, spacing, counts, keep_x, keep_h, w2b, w3b,
    acc1, acc2, acc3, bias,
):
    samples = len(spacing)
    rays = spacing[0].shape[1]
    hidden = w2b.shape[0]
    feat = keep_x.shape[1]
    passed = state[0:1]
    parts = opticals(raw, channels, spacing, counts, samples, rays)
    befores, before = [], None
    for s in range(samples):
        befores.append(before)
        before = parts[s][1] if s == 0 else before + parts[s][1]
    tail = -state[1:2]
    pieces = [None] * samples
    for s in reversed(range(samples)):
        logit, optical, length = parts[s]
        gone = jnp.exp(-optical)
        ahead = 1.0 if s == 0 else jnp.exp(-befores[s])
        weight = ahead * (1.0 - gone)
        color = jax.nn.sigmoid(raw[0:channels, s * rays : (s + 1) * rays])
        weight_grad = passed * jnp.sum(misfit * color, axis=0, keepdims=True)
        optical_grad = weight_grad * (ahead * gone) + tail
        tail = tail - weight_grad * weight
        color_grad = (weight * passed) * misfit * (color * (1.0 - color))
        logit_grad = optical_grad * length * jax.nn.sigmoid(logit)
        row = lax.broadcasted_iota(jnp.int32, (PAD - channels, rays), 0)
        rest = jnp.where(row == 0, jnp.broadcast_to(logit_grad, row.shape), 0.0)
        pieces[s] = jnp.concatenate([color_grad, rest], axis=0)
    draw = jnp.concatenate(pieces, axis=1)
    bias[2 * hidden : 2 * hidden + PAD, :] += lanes(draw)
    dh, dl = split(draw)
    h2h = keep_h[2]
    h2l = keep_h[3]
    both = mm_nt(jnp.concatenate([dh, dl], axis=0), h2h)
    acc3[...] += both[0:PAD] + both[PAD:] + mm_nt(dh, h2l)
    zero = jnp.zeros((256 - 3 * PAD, draw.shape[1]), bf16)
    dh2 = mm(w3b[...], jnp.concatenate([dh, dl, dh, zero], axis=0))
    dz2 = jnp.where(h2h > 0, dh2, 0.0)
    bias[hidden : 2 * hidden, :] += lanes(dz2)
    zh, zl = split(dz2)
    h1h = keep_h[0]
    h1l = keep_h[1]
    acc2[...] += mm_nt(h1h, zh) + mm_nt(h1l, zh) + mm_nt(h1h, zl)
    dh1 = mm(w2b[...], jnp.concatenate([zh, zl, zh], axis=0))
    dz1 = jnp.where(h1h > 0, dh1, 0.0)
    bias[0:hidden, :] += lanes(dz1)
    xh = keep_x[0]
    xl = keep_x[1]
    zh, zl = split(dz1)
    both = mm_nt(jnp.concatenate([xh, xl], axis=0), zh)
    acc1[...] += both[0:feat] + both[feat:] + mm_nt(xh, zl)


def step_kernel(
    views, regions,
    feats, spacing, counts, target, rank_ref, w1, b1, w2, b2, w3, b3,
    pixels, total,
    w1s, w2f, w2b, w3f, w3b, cols, keep_x, keep_h, keep_raw, back, grads,
    acc1, acc2, acc3, bias, fsend, frecv, msend, mrecv, nsend, nrecv, gsend, grecv,
    *scratch,
):
    samples, feat, rays = feats.shape
    channels, seg = target.shape
    levels = regions.bit_length() - 1
    rows = back.shape[1]
    hidden = w2.shape[0]
    me = lax.axis_index("depth")
    view = lax.axis_index("view")
    vlevels = views.bit_length() - 1
    work = scratch[0 : levels + 1]
    got = scratch[levels + 1 : 2 * levels + 1]
    notes = scratch[2 * levels + 1 : 3 * levels + 1]
    sums = scratch[3 * levels + 1 :]

    def bit_of(value, b):
        return lax.rem(value // (1 << b), 2)

    def partner(b):
        return {"depth": me + (1 - 2 * bit_of(me, b)) * (1 << b)}

    def view_partner(b):
        return {"view": view + (1 - 2 * bit_of(view, b)) * (1 << b)}

    def peer(r):
        return {"depth": lax.rem(me + r, regions)}

    barrier = pltpu.get_barrier_semaphore()
    for b in range(vlevels):
        pl.semaphore_signal(barrier, inc=1, device_id=view_partner(b), device_id_type=MESH)
    for r in range(1, regions):
        pl.semaphore_signal(barrier, inc=1, device_id=peer(r), device_id_type=MESH)

    prepare(feat, w1, b1, w2, b2, w3, b3, w1s, w2f, w2b, w3f, w3b, cols)
    pl.semaphore_wait(barrier, vlevels + regions - 1)

    def span_of(k):
        where = 0
        for b in range(levels):
            where = where + lax.rem(bit_of(me, b) + bit_of(k, levels - 1 - b), 2) * (1 << b)
        return pl.ds(pl.multiple_of(where * seg, seg), seg)

    rank = rank_ref[0:1, 0:1]

    def first(b):
        return lax.rem(lax.div(rank, jnp.full_like(rank, 1 << b)), jnp.full_like(rank, 2)) == 0

    def color_copy(j, kk):
        n2 = regions >> (j + 1)
        return remote(work[j].at[n2 + kk], got[j].at[kk], (fsend, frecv), n2 + kk, partner(j))

    def misfit_copy(j, kk):
        n2 = regions >> (j + 1)
        part = pl.ds(0, channels)
        return remote(
            back.at[kk, part], back.at[n2 + kk, part], (msend, mrecv), n2 + kk, partner(j)
        )

    def note_copy(j, kk):
        n2 = regions >> (j + 1)
        return remote(
            notes[j].at[kk], back.at[n2 + kk, pl.ds(channels, rows - channels)],
            (nsend, nrecv), n2 + kk, partner(j),
        )

    def gather_x(span):
        return jnp.concatenate([feats[s, :, span] for s in range(samples)], axis=1)

    def forward_step(i, carry):
        k = regions - 1 - i
        span = span_of(k)
        color, depth = forward_tile(
            feat, channels, gather_x(span), [spacing[s, :, span] for s in range(samples)], counts[:, span],
            w1s, w2f, w3f, cols, keep_x.at[k], keep_h.at[k], keep_raw.at[k],
        )
        work[0][k, 0:channels] = color
        work[0][k, channels:rows] = jnp.broadcast_to(depth, (rows - channels, seg))
        for j in range(levels):
            n2 = regions >> (j + 1)

            @pl.when((k >= n2) & (k < 2 * n2))
            def _():
                color_copy(j, k - n2).start()

            @pl.when(k < n2)
            def _():
                color_copy(j, k).wait_recv()
                ahead = first(j)
                mine, other = work[j][k], got[j][k]
                mine_depth = mine[channels : channels + 1]
                other_depth = other[channels : channels + 1]
                mine_clear = jnp.where(ahead, 1.0, jnp.exp(-other_depth))
                other_clear = jnp.where(ahead, jnp.exp(-mine_depth), 1.0)
                work[j + 1][k, 0:channels] = (
                    mine_clear * mine[0:channels] + other_clear * other[0:channels]
                )
                work[j + 1][k, channels:rows] = mine[channels:rows] + other[channels:rows]

        return carry

    lax.fori_loop(0, regions, forward_step, 0)
    color = work[levels][0, 0:channels]
    pixels[...] = color
    row = lax.broadcasted_iota(jnp.int32, (rows - channels, seg), 0)
    back[0, 0:channels] = color - target[...]
    back[0, channels:rows] = jnp.where(row == 0, 1.0, 0.0)
    for acc in (acc1, acc2, acc3, bias):
        acc[...] = jnp.zeros_like(acc)
    order = sorted(range(regions), key=lambda k: (bin(k).count("1"), -k))

    def backward_step(i, carry):
        k = 0
        for at, value in enumerate(order):
            k = k + jnp.where(i == at, value, 0)
        for j in range(levels):
            n2 = regions >> (j + 1)

            @pl.when((k >= n2) & (k < 2 * n2))
            def _():
                misfit_copy(j, k - n2).wait_recv()
                note_copy(j, k - n2).wait_recv()

        for j in reversed(range(levels)):
            n2 = regions >> (j + 1)

            @pl.when(k < n2)
            def _():
                misfit_copy(j, k).start()

        for j in reversed(range(levels)):
            n2 = regions >> (j + 1)

            @pl.when(k < n2)
            def _():
                ahead = first(j)
                mine, other = work[j][k], got[j][k]
                misfit = back[k, 0:channels]
                state = back[k, channels:rows]
                passed, behind = state[0:1], state[1:2]
                mine_depth = mine[channels : channels + 1]
                other_depth = other[channels : channels + 1]
                hind = jnp.where(ahead, other[0:channels], mine[0:channels])
                later = passed * jnp.exp(-jnp.where(ahead, mine_depth, other_depth))
                glow = behind + later * jnp.sum(misfit * hind, axis=0, keepdims=True)
                mine_state = (jnp.where(ahead, passed, later), jnp.where(ahead, glow, behind))
                other_state = (jnp.where(ahead, later, passed), jnp.where(ahead, behind, glow))
                notes[j][k] = jnp.where(row == 0, *other_state)
                note_copy(j, k).start()
                back[k, channels:rows] = jnp.where(row == 0, *mine_state)

        span = span_of(k)
        backward_tile(
            channels, keep_raw[k], back[k, 0:channels], back[k, channels:rows],
            [spacing[s, :, span] for s in range(samples)], counts[:, span], keep_x.at[k], keep_h.at[k], w2b, w3b,
            acc1, acc2, acc3, bias,
        )
        return carry

    lax.fori_loop(0, regions, backward_step, 0)
    for j in range(levels):
        n2 = regions >> (j + 1)
        for kk in range(n2):
            color_copy(j, kk).wait_send()
            misfit_copy(j, kk).wait_send()
            note_copy(j, kk).wait_send()

    at = 0
    for acc in (acc2, acc1, acc3):
        blocks = acc.shape[0] // 8
        for lane in range(0, hidden, 128):
            grads[at : at + blocks] = acc[:, lane : lane + 128].reshape(blocks, 8, 128)
            at += blocks
    grads[at:] = jnp.zeros((grads.shape[0] - at, 8, 128), f32)
    added = jnp.sum(bias[...].T, axis=0, keepdims=True)
    for lane in range(5):
        grads[at, lane : lane + 1, :] = added[:, lane * 128 : (lane + 1) * 128]

    blocks = grads.shape[0]
    slots = iter(range(10000))
    sems = (gsend, grecv)
    held = grads
    starts = [0]
    for b in range(vlevels):
        size = blocks >> (b + 1)
        copy = remote(
            held.at[pl.ds((1 - bit_of(view, b)) * size, size)],
            sums[2 * b], sems, next(slots), view_partner(b),
        )
        copy.start()
        copy.wait()
        sums[2 * b + 1][...] = held[pl.ds(bit_of(view, b) * size, size)] + sums[2 * b][...]
        held = sums[2 * b + 1]
        starts.append(starts[-1] + bit_of(view, b) * size)
    size = blocks // (views * regions)
    landing = sums[2 * vlevels]
    copies = []
    for r in range(1, regions):
        to = lax.rem(me + r, regions)
        copy = remote(
            held.at[pl.ds(to * size, size)], landing.at[r - 1], sems, next(slots), peer(r)
        )
        copy.start()
        copies.append(copy)
    mine = held[pl.ds(me * size, size)]
    for copy in copies:
        copy.wait()
    for r in range(1, regions):
        mine = mine + landing[r - 1]
    spot = pl.ds(starts[-1] + me * size, size)
    total[spot] = mine
    copies = []
    for r in range(1, regions):
        copy = remote(total.at[spot], total.at[spot], sems, next(slots), peer(r))
        copy.start()
        copies.append(copy)
    for copy in copies:
        copy.wait()
    for b in reversed(range(vlevels)):
        size = blocks >> (b + 1)
        spot = pl.ds(starts[b + 1], size)
        copy = remote(total.at[spot], total.at[spot], sems, next(slots), view_partner(b))
        copy.start()
        copy.wait()


def whole_step(views, regions, feats, spacing, counts, target, rank, weights):
    samples, feat, rays = feats.shape
    channels, seg = target.shape
    hidden = weights[2].shape[0]
    levels = regions.bit_length() - 1
    vlevels = views.bit_length() - 1
    rows = channels + 8
    wide = samples * seg
    blocks = block_count(feat, hidden, views * regions)
    size = blocks // (views * regions)
    scratch = [
        pltpu.VMEM((hidden, 128), bf16),
        pltpu.VMEM((hidden, 3 * hidden), bf16),
        pltpu.VMEM((hidden, 3 * hidden), bf16),
        pltpu.VMEM((2 * PAD, hidden), bf16),
        pltpu.VMEM((hidden, 256), bf16),
        pltpu.VMEM((hidden, hidden), f32),
        pltpu.VMEM((regions, 2, feat, wide), bf16),
        pltpu.VMEM((regions, 4, hidden, wide), bf16),
        pltpu.VMEM((regions, PAD, wide), f32),
        pltpu.VMEM((regions, rows, seg), f32),
        pltpu.VMEM((blocks, 8, 128), f32),
        pltpu.VMEM((feat, hidden), f32),
        pltpu.VMEM((hidden, hidden), f32),
        pltpu.VMEM((PAD, hidden), f32),
        pltpu.VMEM((3 * hidden, 128), f32),
    ]
    scratch += [pltpu.SemaphoreType.DMA((regions,))] * 6
    scratch += [pltpu.SemaphoreType.DMA((2 * (vlevels + regions - 1),))] * 2
    scratch += [pltpu.VMEM((regions >> j, rows, seg), f32) for j in range(levels + 1)]
    scratch += [pltpu.VMEM((regions >> (j + 1), rows, seg), f32) for j in range(levels)]
    scratch += [pltpu.VMEM((regions >> (j + 1), 8, seg), f32) for j in range(levels)]
    for b in range(vlevels):
        scratch += [pltpu.VMEM((blocks >> (b + 1), 8, 128), f32)] * 2
    scratch.append(pltpu.VMEM((regions - 1, size, 8, 128), f32))
    vmem = pl.BlockSpec(memory_space=pltpu.VMEM)
    return pl.pallas_call(
        functools.partial(step_kernel, views, regions),
        in_specs=[vmem] * 11,
        out_specs=[vmem] * 2,
        out_shape=[
            jax.ShapeDtypeStruct((channels, seg), f32),
            jax.ShapeDtypeStruct((blocks, 8, 128), f32),
        ],
        scratch_shapes=scratch,
        compiler_params=pltpu.CompilerParams(
            collective_id=0, has_side_effects=True, vmem_limit_bytes=66000000
        ),
        name="whole_step",
    )(feats, spacing, counts, target, rank, *weights)


def finish_kernel(
    feat, hidden, outs,
    pixels_in, total,
    pixels, first_update, first_shift, second_update, second_shift, last_update, last_shift,
):
    def scaled(value, count):
        square = jnp.sum(jnp.sum(value * value, axis=0, keepdims=True), axis=1, keepdims=True)
        return value / jnp.sqrt(square / count + epsilon)

    pixels[...] = pixels_in[...]
    at = 0
    wholes = []
    for rows in (hidden, feat, PAD):
        halves = []
        for _ in range(0, hidden, 128):
            halves.append(total[at : at + rows // 8].reshape(rows, 128))
            at += rows // 8
        wholes.append(jnp.concatenate(halves, axis=1))
    second_update[...] = scaled(wholes[0], hidden * hidden)
    first_update[...] = scaled(wholes[1], feat * hidden)
    last_update[...] = scaled(wholes[2], hidden * outs)[0:outs]
    rows = total[at]
    first_shift[...] = scaled(jnp.concatenate([rows[0:1], rows[1:2]], axis=1), hidden)
    second_shift[...] = scaled(jnp.concatenate([rows[2:3], rows[3:4]], axis=1), hidden)
    last_shift[...] = scaled(rows[4:5], outs)[:, 0:outs]


def finish(pixels, total, feat, hidden, outs):
    vmem = pl.BlockSpec(memory_space=pltpu.VMEM)
    shapes = [
        pixels.shape, (feat, hidden), (1, hidden), (hidden, hidden), (1, hidden),
        (outs, hidden), (1, outs),
    ]
    return pl.pallas_call(
        functools.partial(finish_kernel, feat, hidden, outs),
        in_specs=[vmem] * 2,
        out_specs=[vmem] * len(shapes),
        out_shape=[jax.ShapeDtypeStruct(shape, f32) for shape in shapes],
        name="normalize_all",
    )(pixels, total)


def local(
    features, spacing, counts, depth_rank, target,
    first_weight, first_bias, second_weight, second_bias, last_weight, last_bias,
):
    regions = lax.axis_size("depth")
    views = lax.axis_size("view")
    feat, hidden = first_weight.shape
    outs = last_weight.shape[1]
    feats, gaps, live = jnp.transpose(features[0, 0], (1, 0, 2)), jnp.transpose(spacing[0], (1, 0, 2)), counts[0]
    weights = (
        first_weight, first_bias[None], second_weight, second_bias[None],
        last_weight.T, last_bias[None],
    )
    pixels, total = whole_step(views, regions, feats, gaps, live, target[0], depth_rank, weights)
    results = finish(pixels, total, feat, hidden, outs)
    return (
        results[0][None], results[1], results[2][0], results[3], results[4][0],
        results[5].T, results[6][0],
    )


def solution(mesh):
    return jax.shard_map(
        local,
        mesh=mesh,
        in_specs=(
            P("view", "depth", None, None, None),
            P("view", "depth", None, None),
            P("view", "depth", None),
            P("view", "depth"),
            P("view", None, "depth"),
            P(), P(), P(), P(), P(), P(),
        ),
        out_specs=(P("view", None, "depth"), P(), P(), P(), P(), P(), P()),
        check_vma=False,
    )
```

profile of v0, /device:TPU:0, one launch (start us, length us, event | category | flops | bytes accessed | tf_op | source)
XLA Modules:
  0.0 83.9 jit_solution(7972999572217848945)
XLA Ops:
  1.3 80.6 %whole_step.1 = (f32[64,512]{1,0:T(8,128)}, f32[96,8,128]{2,1,0:T(8,128)}) custom-call(f32[3,32,4096]{2,1,0:T(8,128)} %bitcast.15, f32[3,1,4096]{2,1,0:T(1,128)} %bitcast.18, s32[1,4096]{1,0:T(1,128)} %bitcast.19, f32[64,512]{1,0:T(8,128)} %bitcast.16, s32[1,1]{1,0:T(1,128)S(6)} %copy.18.rank_ref, f32[32,256]{1,0:T(8,128)} %w1.1, f32[1,256]{1,0:T(1,128)} %bitcast.20, ...), custom_call_target="tpu_custom_call" | custom-call | tf_op jit(solution)/shard_map/whole_step/pallas_call | solution.py:455
  81.9 2.0 %normalize_all.1 = (f32[64,512]{1,0:T(8,128)}, f32[32,256]{1,0:T(8,128)}, f32[1,256]{1,0:T(1,128)}, f32[256,256]{1,0:T(8,128)}, f32[1,256]{1,0:T(1,128)}, /*index=5*/f32[65,256]{1,0:T(8,128)}, f32[1,65]{1,0:T(1,128)}) custom-call(f32[64,512]{1,0:T(8,128)} %get-tuple-element.16.pixels_in, f32[96,8,128]{2,1,0:T(8,128)} %get-tuple-element.17.total), custom_call_target="tpu_custom_call" | custom-call | tf_op jit(solution)/shard_map/normalize_all/pallas_call | solution.py:504
where the time goes:
time: 84.1 us; the launch traced here: 83.9 us
  Pallas kernels  82.6 us (98%)
  between operations  1.29 us (2%)
    pallas_call x1, Pallas kernels, whole_step(): pl.pallas_call(functools.partial(step_kernel, views, regions), in_specs=[...  80.6 us
    pallas_call x1, Pallas kernels, finish(): pl.pallas_call(functools.partial(finish_kernel, feat, hidden, outs), in_s...  1.96 us

commit v1 on v0

--- a/solution.py
+++ b/solution.py
@@ -56,9 +56,113 @@
     return total
 
 
-def block_count(feat, hidden, devices):
-    blocks = (hidden + feat + PAD) // 8 * (hidden // 128) + 1
+def round_up(blocks, devices):
     return -(-blocks // devices) * devices
+
+
+def block_counts(feat, hidden, devices):
+    across = hidden // 128
+    late = feat // 8 * across + 1
+    early = (hidden + PAD) // 8 * across + 1
+    return round_up(early, devices), round_up(late, devices)
+
+
+def fill(grads, accs, rows):
+    at = 0
+    for acc in accs:
+        blocks = acc.shape[0] // 8
+        for lane in range(0, acc.shape[1], 128):
+            grads[at : at + blocks] = acc[:, lane : lane + 128].reshape(blocks, 8, 128)
+            at += blocks
+    grads[at:] = jnp.zeros((grads.shape[0] - at, 8, 128), f32)
+    added = jnp.sum(rows.T, axis=0, keepdims=True)
+    for i, lane in enumerate(range(0, rows.shape[0], 128)):
+        grads[at, i : i + 1, :] = added[:, lane : lane + 128]
+
+
+def total_stages(views, regions, grads, total, sums, sems):
+    me = lax.axis_index("depth")
+    view = lax.axis_index("view")
+    vlevels = views.bit_length() - 1
+    blocks = grads.shape[0]
+    small = blocks // (views * regions)
+    landing = sums[2 * vlevels]
+
+    def bit_of(b):
+        return lax.rem(view // (1 << b), 2)
+
+    def view_partner(b):
+        return {"view": view + (1 - 2 * bit_of(b)) * (1 << b)}
+
+    def peer(r):
+        return {"depth": lax.rem(me + r, regions)}
+
+    def held(b):
+        return grads if b == 0 else sums[2 * b - 1]
+
+    def base(b):
+        start = 0
+        for c in range(b):
+            start = start + bit_of(c) * (blocks >> (c + 1))
+        return start
+
+    def scatter_view(b):
+        size = blocks >> (b + 1)
+        part = pl.ds((1 - bit_of(b)) * size, size)
+        return [remote(held(b).at[part], sums[2 * b], sems, b, view_partner(b))]
+
+    def add_view(b):
+        size = blocks >> (b + 1)
+        sums[2 * b + 1][...] = held(b)[pl.ds(bit_of(b) * size, size)] + sums[2 * b][...]
+
+    def scatter_depth():
+        return [
+            remote(
+                held(vlevels).at[pl.ds(lax.rem(me + r, regions) * small, small)],
+                landing.at[r - 1], sems, vlevels + r - 1, peer(r),
+            )
+            for r in range(1, regions)
+        ]
+
+    def spot():
+        return pl.ds(base(vlevels) + me * small, small)
+
+    def add_depth():
+        mine = held(vlevels)[pl.ds(me * small, small)]
+        for r in range(1, regions):
+            mine = mine + landing[r - 1]
+        total[spot()] = mine
+
+    def gather_depth():
+        part = total.at[spot()]
+        first = vlevels + regions - 1
+        return [remote(part, part, sems, first + r - 1, peer(r)) for r in range(1, regions)]
+
+    def gather_view(b):
+        part = total.at[pl.ds(base(b + 1), blocks >> (b + 1))]
+        slot = vlevels + 2 * (regions - 1) + b
+        return [remote(part, part, sems, slot, view_partner(b))]
+
+    moves = [
+        (functools.partial(scatter_view, b), functools.partial(add_view, b))
+        for b in range(vlevels)
+    ]
+    moves.append((scatter_depth, add_depth))
+    moves.append((gather_depth, None))
+    moves += [(functools.partial(gather_view, b), None) for b in reversed(range(vlevels))]
+
+    def stage(n):
+        if n > 0:
+            copies, after = moves[n - 1]
+            for copy in copies():
+                copy.wait()
+            if after is not None:
+                after()
+        if n < len(moves):
+            for copy in moves[n][0]():
+                copy.start()
+
+    return [functools.partial(stage, n) for n in range(len(moves) + 1)]
 
 
 def prepare(feat, w1_ref, b1_ref, w2_ref, b2_ref, w3_ref, b3_ref, w1s, w2f, w2b, w3f, w3b, cols):
@@ -131,13 +235,11 @@
 
 
 def backward_tile(
-    channels, raw, misfit, state, spacing, counts, keep_x, keep_h, w2b, w3b,
-    acc1, acc2, acc3, bias,
+    channels, raw, misfit, state, spacing, counts, keep_h, w3b, acc2, acc3, bias,
 ):
     samples = len(spacing)
     rays = spacing[0].shape[1]
-    hidden = w2b.shape[0]
-    feat = keep_x.shape[1]
+    hidden = w3b.shape[0]
     passed = state[0:1]
     parts = opticals(raw, channels, spacing, counts, samples, rays)
     befores, before = [], None
@@ -174,7 +276,18 @@
     zh, zl = split(dz2)
     h1h = keep_h[0]
     h1l = keep_h[1]
-    acc2[...] += mm_nt(h1h, zh) + mm_nt(h1l, zh) + mm_nt(h1h, zl)
+    both = mm_nt(jnp.concatenate([h1h, h1l], axis=0), zh)
+    acc2[...] += both[0:hidden] + both[hidden:] + mm_nt(h1h, zl)
+    keep_h[2] = zh
+    keep_h[3] = zl
+
+
+def first_layer_tile(keep_x, keep_h, w2b, acc1, bias):
+    hidden = w2b.shape[0]
+    feat = keep_x.shape[1]
+    h1h = keep_h[0]
+    zh = keep_h[2]
+    zl = keep_h[3]
     dh1 = mm(w2b[...], jnp.concatenate([zh, zl, zh], axis=0))
     dz1 = jnp.where(h1h > 0, dh1, 0.0)
     bias[0:hidden, :] += lanes(dz1)
@@ -188,9 +301,9 @@
 def step_kernel(
     views, regions,
     feats, spacing, counts, target, rank_ref, w1, b1, w2, b2, w3, b3,
-    pixels, total,
-    w1s, w2f, w2b, w3f, w3b, cols, keep_x, keep_h, keep_raw, back, grads,
-    acc1, acc2, acc3, bias, fsend, frecv, msend, mrecv, nsend, nrecv, gsend, grecv,
+    pixels, total, total_late,
+    w1s, w2f, w2b, w3f, w3b, cols, keep_x, keep_h, keep_raw, back, grads, grads_late,
+    acc1, acc2, acc3, bias, fsend, frecv, msend, mrecv, nsend, nrecv, gsend, grecv, lsend, lrecv,
     *scratch,
 ):
     samples, feat, rays = feats.shape
@@ -300,11 +413,19 @@
     for acc in (acc1, acc2, acc3, bias):
         acc[...] = jnp.zeros_like(acc)
     order = sorted(range(regions), key=lambda k: (bin(k).count("1"), -k))
-
-    def backward_step(i, carry):
+    if regions >= 8:
+        order = [{3: 5, 5: 3}.get(k, k) for k in order]
+
+    def tile_at(i):
         k = 0
         for at, value in enumerate(order):
             k = k + jnp.where(i == at, value, 0)
+        return k
+
+    defer = regions // 2
+
+    def backward_step(i, carry):
+        k = tile_at(i)
         for j in range(levels):
             n2 = regions >> (j + 1)
 
@@ -344,9 +465,14 @@
         span = span_of(k)
         backward_tile(
             channels, keep_raw[k], back[k, 0:channels], back[k, channels:rows],
-            [spacing[s, :, span] for s in range(samples)], counts[:, span], keep_x.at[k], keep_h.at[k], w2b, w3b,
-            acc1, acc2, acc3, bias,
+            [spacing[s, :, span] for s in range(samples)], counts[:, span], keep_h.at[k], w3b,
+            acc2, acc3, bias,
         )
+
+        @pl.when(i < defer)
+        def _():
+            first_layer_tile(keep_x.at[k], keep_h.at[k], w2b, acc1, bias)
+
         return carry
 
     lax.fori_loop(0, regions, backward_step, 0)
@@ -357,63 +483,29 @@
             misfit_copy(j, kk).wait_send()
             note_copy(j, kk).wait_send()
 
-    at = 0
-    for acc in (acc2, acc1, acc3):
-        blocks = acc.shape[0] // 8
-        for lane in range(0, hidden, 128):
-            grads[at : at + blocks] = acc[:, lane : lane + 128].reshape(blocks, 8, 128)
-            at += blocks
-    grads[at:] = jnp.zeros((grads.shape[0] - at, 8, 128), f32)
-    added = jnp.sum(bias[...].T, axis=0, keepdims=True)
-    for lane in range(5):
-        grads[at, lane : lane + 1, :] = added[:, lane * 128 : (lane + 1) * 128]
-
-    blocks = grads.shape[0]
-    slots = iter(range(10000))
-    sems = (gsend, grecv)
-    held = grads
-    starts = [0]
-    for b in range(vlevels):
-        size = blocks >> (b + 1)
-        copy = remote(
-            held.at[pl.ds((1 - bit_of(view, b)) * size, size)],
-            sums[2 * b], sems, next(slots), view_partner(b),
-        )
-        copy.start()
-        copy.wait()
-        sums[2 * b + 1][...] = held[pl.ds(bit_of(view, b) * size, size)] + sums[2 * b][...]
-        held = sums[2 * b + 1]
-        starts.append(starts[-1] + bit_of(view, b) * size)
-    size = blocks // (views * regions)
-    landing = sums[2 * vlevels]
-    copies = []
-    for r in range(1, regions):
-        to = lax.rem(me + r, regions)
-        copy = remote(
-            held.at[pl.ds(to * size, size)], landing.at[r - 1], sems, next(slots), peer(r)
-        )
-        copy.start()
-        copies.append(copy)
-    mine = held[pl.ds(me * size, size)]
-    for copy in copies:
-        copy.wait()
-    for r in range(1, regions):
-        mine = mine + landing[r - 1]
-    spot = pl.ds(starts[-1] + me * size, size)
-    total[spot] = mine
-    copies = []
-    for r in range(1, regions):
-        copy = remote(total.at[spot], total.at[spot], sems, next(slots), peer(r))
-        copy.start()
-        copies.append(copy)
-    for copy in copies:
-        copy.wait()
-    for b in reversed(range(vlevels)):
-        size = blocks >> (b + 1)
-        spot = pl.ds(starts[b + 1], size)
-        copy = remote(total.at[spot], total.at[spot], sems, next(slots), view_partner(b))
-        copy.start()
-        copy.wait()
+    count = 2 * vlevels + 1
+    early = total_stages(views, regions, grads, total, sums[0:count], (gsend, grecv))
+    late = total_stages(views, regions, grads_late, total_late, sums[count:], (lsend, lrecv))
+    fill(grads, (acc2, acc3), bias[hidden:, :])
+    early[0]()
+
+    def first_layer_step(i, carry):
+        k = tile_at(i)
+        first_layer_tile(keep_x.at[k], keep_h.at[k], w2b, acc1, bias)
+
+        @pl.when(i == defer)
+        def _():
+            early[1]()
+
+        return carry
+
+    lax.fori_loop(defer, regions, first_layer_step, 0)
+    fill(grads_late, (acc1,), bias[0:hidden, :])
+    early = early[2:]
+    for which in "LELLELELELL" + "EL" * (2 * len(late)):
+        queue = early if which == "E" else late
+        if queue:
+            queue.pop(0)()
 
 
 def whole_step(views, regions, feats, spacing, counts, target, rank, weights):
@@ -424,8 +516,8 @@
     vlevels = views.bit_length() - 1
     rows = channels + 8
     wide = samples * seg
-    blocks = block_count(feat, hidden, views * regions)
-    size = blocks // (views * regions)
+    devices = views * regions
+    sizes = block_counts(feat, hidden, devices)
     scratch = [
         pltpu.VMEM((hidden, 128), bf16),
         pltpu.VMEM((hidden, 3 * hidden), bf16),
@@ -437,28 +529,31 @@
         pltpu.VMEM((regions, 4, hidden, wide), bf16),
         pltpu.VMEM((regions, PAD, wide), f32),
         pltpu.VMEM((regions, rows, seg), f32),
-        pltpu.VMEM((blocks, 8, 128), f32),
+        pltpu.VMEM((sizes[0], 8, 128), f32),
+        pltpu.VMEM((sizes[1], 8, 128), f32),
         pltpu.VMEM((feat, hidden), f32),
         pltpu.VMEM((hidden, hidden), f32),
         pltpu.VMEM((PAD, hidden), f32),
         pltpu.VMEM((3 * hidden, 128), f32),
     ]
     scratch += [pltpu.SemaphoreType.DMA((regions,))] * 6
-    scratch += [pltpu.SemaphoreType.DMA((2 * (vlevels + regions - 1),))] * 2
+    scratch += [pltpu.SemaphoreType.DMA((2 * (vlevels + regions - 1),))] * 4
     scratch += [pltpu.VMEM((regions >> j, rows, seg), f32) for j in range(levels + 1)]
     scratch += [pltpu.VMEM((regions >> (j + 1), rows, seg), f32) for j in range(levels)]
     scratch += [pltpu.VMEM((regions >> (j + 1), 8, seg), f32) for j in range(levels)]
-    for b in range(vlevels):
-        scratch += [pltpu.VMEM((blocks >> (b + 1), 8, 128), f32)] * 2
-    scratch.append(pltpu.VMEM((regions - 1, size, 8, 128), f32))
+    for blocks in sizes:
+        for b in range(vlevels):
+            scratch += [pltpu.VMEM((blocks >> (b + 1), 8, 128), f32)] * 2
+        scratch.append(pltpu.VMEM((regions - 1, blocks // devices, 8, 128), f32))
     vmem = pl.BlockSpec(memory_space=pltpu.VMEM)
     return pl.pallas_call(
         functools.partial(step_kernel, views, regions),
         in_specs=[vmem] * 11,
-        out_specs=[vmem] * 2,
+        out_specs=[vmem] * 3,
         out_shape=[
             jax.ShapeDtypeStruct((channels, seg), f32),
-            jax.ShapeDtypeStruct((blocks, 8, 128), f32),
+            jax.ShapeDtypeStruct((sizes[0], 8, 128), f32),
+            jax.ShapeDtypeStruct((sizes[1], 8, 128), f32),
         ],
         scratch_shapes=scratch,
         compiler_params=pltpu.CompilerParams(
@@ -470,7 +565,7 @@
 
 def finish_kernel(
     feat, hidden, outs,
-    pixels_in, total,
+    pixels_in, total, late,
     pixels, first_update, first_shift, second_update, second_shift, last_update, last_shift,
 ):
     def scaled(value, count):
@@ -478,24 +573,30 @@
         return value / jnp.sqrt(square / count + epsilon)
 
     pixels[...] = pixels_in[...]
-    at = 0
-    wholes = []
-    for rows in (hidden, feat, PAD):
+
+    def join(source, at, rows):
         halves = []
         for _ in range(0, hidden, 128):
-            halves.append(total[at : at + rows // 8].reshape(rows, 128))
+            halves.append(source[at : at + rows // 8].reshape(rows, 128))
             at += rows // 8
-        wholes.append(jnp.concatenate(halves, axis=1))
-    second_update[...] = scaled(wholes[0], hidden * hidden)
-    first_update[...] = scaled(wholes[1], feat * hidden)
-    last_update[...] = scaled(wholes[2], hidden * outs)[0:outs]
+        return jnp.concatenate(halves, axis=1), at
+
+    second, at = join(total, 0, hidden)
+    last, at = join(total, at, PAD)
+    first, late_at = join(late, 0, feat)
+    second_update[...] = scaled(second, hidden * hidden)
+    first_update[...] = scaled(first, feat * hidden)
+    last_update[...] = scaled(last, hidden * outs)[0:outs]
+    across = hidden // 128
     rows = total[at]
-    first_shift[...] = scaled(jnp.concatenate([rows[0:1], rows[1:2]], axis=1), hidden)
-    second_shift[...] = scaled(jnp.concatenate([rows[2:3], rows[3:4]], axis=1), hidden)
-    last_shift[...] = scaled(rows[4:5], outs)[:, 0:outs]
-
-
-def finish(pixels, total, feat, hidden, outs):
+    late_rows = late[late_at]
+    wide = lambda rows: jnp.concatenate([rows[i : i + 1] for i in range(across)], axis=1)
+    first_shift[...] = scaled(wide(late_rows), hidden)
+    second_shift[...] = scaled(wide(rows), hidden)
+    last_shift[...] = scaled(rows[across : across + 1], outs)[:, 0:outs]
+
+
+def finish(pixels, total, late, feat, hidden, outs):
     vmem = pl.BlockSpec(memory_space=pltpu.VMEM)
     shapes = [
         pixels.shape, (feat, hidden), (1, hidden), (hidden, hidden), (1, hidden),
@@ -503,11 +604,11 @@
     ]
     return pl.pallas_call(
         functools.partial(finish_kernel, feat, hidden, outs),
-        in_specs=[vmem] * 2,
+        in_specs=[vmem] * 3,
         out_specs=[vmem] * len(shapes),
         out_shape=[jax.ShapeDtypeStruct(shape, f32) for shape in shapes],
         name="normalize_all",
-    )(pixels, total)
+    )(pixels, total, late)
 
 
 def local(
@@ -523,8 +624,8 @@
         first_weight, first_bias[None], second_weight, second_bias[None],
         last_weight.T, last_bias[None],
     )
-    pixels, total = whole_step(views, regions, feats, gaps, live, target[0], depth_rank, weights)
-    results = finish(pixels, total, feat, hidden, outs)
+    pixels, total, late = whole_step(views, regions, feats, gaps, live, target[0], depth_rank, weights)
+    results = finish(pixels, total, late, feat, hidden, outs)
     return (
         results[0][None], results[1], results[2][0], results[3], results[4][0],
         results[5].T, results[6][0],

time: 84.1 us -> 79.8 us (0.949)
  Pallas kernels: 82.6 us -> 78.3 us
    pallas_call x1, Pallas kernels: 80.6 us -> 76.4 us  [whole_step(): pl.pallas_call(functools.partial(step_kernel, views, regions), in_specs=[...]
where the time goes in v1:
time: 79.8 us; the launch traced here: 79.6 us
  Pallas kernels  78.3 us (98%)
  between operations  1.29 us (2%)
    pallas_call x1, Pallas kernels, whole_step(): pl.pallas_call(functools.partial(step_kernel, views, regions), in_specs=[...  76.4 us
    pallas_call x1, Pallas kernels, finish(): pl.pallas_call(functools.partial(finish_kernel, feat, hidden, outs), in_s...  1.97 us

profile of v1, /device:TPU:0, one launch (start us, length us, event | category | flops | bytes accessed | tf_op | source)
XLA Modules:
  0.0 79.6 jit_solution(5021184741353731859)
XLA Ops:
  1.3 76.4 %whole_step.1 = (f32[64,512]{1,0:T(8,128)}, f32[96,8,128]{2,1,0:T(8,128)}, f32[32,8,128]{2,1,0:T(8,128)}) custom-call(f32[3,32,4096]{2,1,0:T(8,128)} %bitcast.15, f32[3,1,4096]{2,1,0:T(1,128)} %bitcast.18, s32[1,4096]{1,0:T(1,128)} %bitcast.19, f32[64,512]{1,0:T(8,128)} %bitcast.16, s32[1,1]{1,0:T(1,128)S(6)} %copy.18.rank_ref, f32[32,256]{1,0:T(8,128)} %w1.1, ...), custom_call_target="tpu_custom_call" | custom-call | tf_op jit(solution)/shard_map/whole_step/pallas_call | solution.py:549
  77.7 2.0 %normalize_all.1 = (f32[64,512]{1,0:T(8,128)}, f32[32,256]{1,0:T(8,128)}, f32[1,256]{1,0:T(1,128)}, f32[256,256]{1,0:T(8,128)}, f32[1,256]{1,0:T(1,128)}, /*index=5*/f32[65,256]{1,0:T(8,128)}, f32[1,65]{1,0:T(1,128)}) custom-call(f32[64,512]{1,0:T(8,128)} %get-tuple-element.17.pixels_in, f32[96,8,128]{2,1,0:T(8,128)} %get-tuple-element.18.total, ...), custom_call_target="tpu_custom_call" | custom-call | tf_op jit(solution)/shard_map/normalize_all/pallas_call | solution.py:605
